TPU v7x, 32 devices: a whole 2x2x4 slice. The times are simulated.
32 devices in a mesh: ens: 2 (over y), row: 4 (over z), col: 2 (over x), chan: 2 (over core).
Axes of the slice: x: 2, y: 2, z: 4, core: 2. Of those that a mesh axis runs over, the one named last changes fastest.
Arguments:
- latent: float32 [4, 12, 32, 256], P('ens', None, 'row', 'col'), parts along dimension 0, may hold values from -6 to 6
- fresh_noise: float32 [4, 12, 32, 256], P('ens', None, 'row', 'col'), parts along dimension 0, may hold values from -6 to 6
- step_index: int32 [4], P('ens'), parts along dimension 0, may hold values from 0 to 11
- coarse: float32 [24, 4, 32], P('ens', None, 'col'), parts along dimension 0, may hold values from -6 to 6
- weight_in: bfloat16 [9, 256, 24], replicated, may hold values from -0.4375 to 0.4375
- bias_in: float32 [256], replicated, may hold values from -4 to 4
- weight_noise: float32 [256], replicated, may hold values from -4 to 4
- weight_mid: bfloat16 [9, 256, 256], P(None, 'chan'), may hold values from -0.125 to 0.125
- bias_mid: float32 [256], P('chan'), may hold values from -4 to 4
- weight_out: bfloat16 [12, 256], P(None, 'chan'), may hold values from -0.375 to 0.375
Outputs:
- fine_field: float32 [4, 12, 32, 256], P('ens', None, 'row', 'col'), parts along dimension 0
- next_latent: float32 [4, 12, 32, 256], P('ens', None, 'row', 'col'), parts along dimension 0
There are 2 independent parts, one for each index of `ens`. A program takes and returns all parts, laid end to end along the dimension named above; an argument that names none is the same for every part. Nothing has to cross between parts.
Inputs may be any that keep to these rules, and one draw needn't show every extreme that they name: `step_index`: each sample's position in the noise plan of 18 steps.
All inputs are finite; a program needn't handle non-finite values.
Results may differ from a plain program's by a relative error of at most 0.0024.
Values may be sent and summed in bfloat16 or wider, within the bound.
No kernel may reach another device: no remote copies, remote signals or barrier semaphores. Data moves between devices by JAX's collectives and lax.ppermute only.
A program may use at most 64 MiB of HBM per device.

v0:
```python
import jax
import jax.numpy as jnp
from jax import lax
from jax.sharding import PartitionSpec as P

STEPS = 18
FACTOR = 8
sigma_data = 0.5
sigma_high = 80.0
sigma_low = 0.002
rho_power = 7.0


def extended_2(value, sides, width):
    for axis, dim in sides:
        count, length = (lax.axis_size(axis), value.shape[dim])
        up = [(i, (i + 1) % count) for i in range(count - 1)]
        down = [(j, i) for i, j in up]
        last = lax.slice_in_dim(value, length - width, length, axis=dim)
        initial = lax.slice_in_dim(value, 0, width, axis=dim)
        before = lax.ppermute(last, axis, up)
        after = lax.ppermute(initial, axis, down)
        value = jnp.concatenate([before, value, after], axis=dim)
    return value


def blend_matrix(fine_index, coarse_index, coarse_count, factor):
    twice_pos = 2 * fine_index + 1 - factor
    lower_cell = twice_pos // (2 * factor)
    fraction = (twice_pos - lower_cell * 2 * factor).astype(jnp.float32) / (2.0 * factor)
    before = lower_cell < 0
    fraction = jnp.where(before, 0.0, fraction)
    lower_clip = jnp.clip(lower_cell, 0, coarse_count - 1)
    upper_clip = jnp.clip(lower_cell + 1, 0, coarse_count - 1)
    lower_hit = (lower_clip[:, None] == coarse_index[None, :]).astype(jnp.float32)
    upper_hit = (upper_clip[:, None] == coarse_index[None, :]).astype(jnp.float32)
    return (1.0 - fraction)[:, None] * lower_hit + fraction[:, None] * upper_hit


def noise_level(position):
    top_root = sigma_high ** (1.0 / rho_power)
    bottom_root = sigma_low ** (1.0 / rho_power)
    along = position.astype(jnp.float32) / (STEPS - 1)
    return (top_root + along * (bottom_root - top_root)) ** rho_power


def conv_valid(source, weight, out_rows, out_cols):
    total = None
    for offset_row in range(3):
        for offset_col in range(3):
            window = source[
                :, :, offset_row : offset_row + out_rows, offset_col : offset_col + out_cols
            ]
            term = jnp.einsum(
                "oi,siyx->soyx",
                weight[3 * offset_row + offset_col],
                window,
                preferred_element_type=jnp.float32,
            )
            total = term if total is None else total + term
    return total


def on_device(
    latent,
    fresh_noise,
    step_index,
    coarse,
    weight_in,
    bias_in,
    weight_noise,
    weight_mid,
    bias_mid,
    weight_out,
):
    samples, channels, rows_here, cols_here = latent.shape
    row_place = lax.axis_index("row")
    col_place = lax.axis_index("col")
    height = lax.axis_size("row") * rows_here
    width = lax.axis_size("col") * cols_here
    coarse_rows = coarse.shape[1]
    local_cols = coarse.shape[2]
    coarse_cols = lax.axis_size("col") * local_cols
    widened = extended_2(coarse, (("col", 2),), 1)
    rows_matrix = blend_matrix(
        row_place * rows_here + jnp.arange(rows_here, dtype=jnp.int32),
        jnp.arange(coarse_rows, dtype=jnp.int32),
        coarse_rows,
        FACTOR,
    )
    cols_matrix = blend_matrix(
        col_place * cols_here + jnp.arange(cols_here, dtype=jnp.int32),
        col_place * local_cols - 1 + jnp.arange(local_cols + 2, dtype=jnp.int32),
        coarse_cols,
        FACTOR,
    )
    mean_up = jnp.einsum(
        "yh,khw,xw->kyx", rows_matrix, widened, cols_matrix, precision=lax.Precision.HIGHEST
    )
    noise_now = noise_level(step_index)
    noise_next = noise_level(step_index + 1)
    inputs = jnp.concatenate(
        [latent, jnp.broadcast_to(mean_up[None], (samples,) + mean_up.shape)], axis=1
    ).astype(jnp.bfloat16)
    conditioning = (
        bias_in[None, :, None, None]
        + (jnp.log(noise_now) / 4.0)[:, None, None, None] * weight_noise[None, :, None, None]
    )
    mid_full, out_full = (
        lax.all_gather(weight_mid, "chan", axis=1, tiled=True),
        lax.all_gather(weight_out, "chan", axis=1, tiled=True),
    )
    bias_full = lax.all_gather(bias_mid, "chan", axis=0, tiled=True)
    half_cols = cols_here // lax.axis_size("chan")
    chan_place = lax.axis_index("chan")
    extended = extended_2(inputs, (("row", 2), ("col", 3)), 2)
    source = lax.dynamic_slice_in_dim(extended, chan_place * half_cols, half_cols + 4, 3)
    hidden = jax.nn.silu(conv_valid(source, weight_in, rows_here + 2, half_cols + 2) + conditioning)
    global_rows = row_place * rows_here - 1 + jnp.arange(rows_here + 2, dtype=jnp.int32)
    global_cols = (
        col_place * cols_here
        + chan_place * half_cols
        - 1
        + jnp.arange(half_cols + 2, dtype=jnp.int32)
    )
    inside = ((global_rows >= 0) & (global_rows < height))[:, None] & (
        (global_cols >= 0) & (global_cols < width)
    )[None, :]
    hidden_wide = jnp.where(inside, hidden, 0.0).astype(jnp.bfloat16)
    middle = jax.nn.silu(
        conv_valid(hidden_wide, mid_full, rows_here, half_cols) + bias_full[None, :, None, None]
    ).astype(jnp.bfloat16)
    half_network = jnp.einsum("ko,soyx->skyx", out_full, middle, preferred_element_type=jnp.float32)
    network = lax.all_gather(half_network, "chan", axis=3, tiled=True)
    scale_now = jnp.sqrt(noise_now * noise_now + sigma_data * sigma_data)
    skip_coef = sigma_data * sigma_data / (noise_now * noise_now + sigma_data * sigma_data)
    out_coef = sigma_data * noise_now / scale_now
    denoised = (skip_coef * scale_now)[:, None, None, None] * latent + out_coef[
        :, None, None, None
    ] * network
    fine_field = mean_up[None] + denoised
    scale_next = jnp.sqrt(noise_next * noise_next + sigma_data * sigma_data)
    next_latent = (denoised + noise_next[:, None, None, None] * fresh_noise) / scale_next[
        :, None, None, None
    ]
    return (fine_field, next_latent)


def solution(mesh):
    in_specs = (
        P("ens", None, "row", "col"),
        P("ens", None, "row", "col"),
        P("ens"),
        P("ens", None, "col"),
        P(),
        P(),
        P(),
        P(None, "chan", None),
        P("chan"),
        P(None, "chan"),
    )
    out_specs = (P("ens", None, "row", "col"), P("ens", None, "row", "col"))
    return jax.shard_map(
        on_device, mesh=mesh, in_specs=in_specs, out_specs=out_specs, check_vma=False
    )
```

profile of v0, /device:TPU:0, one launch (start us, length us, event | category | flops | bytes accessed | tf_op | source)
XLA Modules:
  0.0 60.4 jit_solution(1089614030091482770)
XLA Ops:
  7.2 0.0 copy-start.5
  7.2 0.0 copy-start.4
  7.2 0.0 all-gather.3.cloned.1.call-start
  7.2 0.7 %copy.29 = f32[12,4,16]{2,0,1:T(8,128)S(1)} copy(f32[12,4,16]{2,1,0:T(4,128)} %param.13) | data formatting | bytes 6144 | tf_op args[3]
  8.0 0.1 fusion.95
  8.0 4.9 %collective-permute-start = (f32[12,4,1]{2,0,1:T(8,128)S(1)}, f32[12,4,1]{2,0,1:T(8,128)S(1)}, u32[]{:S(2)}, u32[]{:S(2)}) collective-permute-start(f32[12,4,1]{2,0,1:T(8,128)S(1)} %get-tuple-element.23), channel_id=1, source_target_pairs={{0,2},{1,3},{4,6},{5,7},{8,10},{9,11},{12,14},{13,15},{16,18},{17,... | collective-permute-start | bytes 584 | tf_op jit(solution)/shard_map/ppermute | solution.py:21
  12.9 1.3 %collective-permute-start.1 = (f32[12,4,1]{2,0,1:T(8,128)S(1)}, f32[12,4,1]{2,0,1:T(8,128)S(1)}, u32[]{:S(2)}, u32[]{:S(2)}) collective-permute-start(f32[12,4,1]{2,0,1:T(8,128)S(1)} %get-tuple-element.24), channel_id=1, source_target_pairs={{2,0},{3,1},{6,4},{7,5},{10,8},{11,9},{14,12},{15,13},{18,16},{19,... | collective-permute-start | bytes 584 | tf_op jit(solution)/shard_map/ppermute | solution.py:22
  14.2 0.0 all-gather.3.cloned.1.call-update
  14.4 0.8 %add_sqrt_fusion = (f32[2]{0:T(128)S(1)}, f32[2]{0:T(128)S(1)}, f32[2]{0:T(128)S(1)}, f32[2]{0:T(128)S(1)}, f32[2]{0:T(128)S(1)}) fusion(s32[2]{0:T(128)} %param.12), kind=kLoop, calls=%fused_computation.139 | loop fusion | flops 34 | bytes 48 | tf_op jit(solution)/shard_map/sqrt | solution.py:142
  15.1 0.8 %multiply_add_fusion.1 = f32[2,256]{1,0:T(2,128)S(1)} fusion(f32[256]{0:T(256)} %param.16, f32[256]{0:T(256)} %param.15, f32[2]{0:T(128)S(1)} %get-tuple-element.25), kind=kLoop, calls=%fused_computation.115 | loop fusion | flops 1024 | bytes 4104 | tf_op jit(solution)/shard_map/add | solution.py:106
  15.9 0.9 %convert.7 = bf16[2,12,8,128]{3,2,1,0:T(8,128)(2,1)S(1)} convert(f32[2,12,8,128]{3,2,1,0:T(8,128)} %param.10) | non-fusion elementwise | flops 24576 | bytes 147456 | tf_op jit(solution)/shard_map/convert
  16.8 0.0 collective-permute-done
  16.8 1.9 %collective-permute-done.1 = f32[12,4,1]{2,0,1:T(8,128)S(1)} collective-permute-done((f32[12,4,1]{2,0,1:T(8,128)S(1)}, f32[12,4,1]{2,0,1:T(8,128)S(1)}, u32[]{:S(2)}, u32[]{:S(2)}) %collective-permute-start.1) | collective-permute-done | bytes 224 | tf_op jit(solution)/shard_map/ppermute | solution.py:22
  18.7 0.2 fusion.42
  19.0 0.2 fusion.96
  19.3 3.5 %collective-permute-start.2 = (bf16[2,24,2,128]{3,2,1,0:T(2,128)(2,1)S(1)}, bf16[2,24,2,128]{3,2,1,0:T(2,128)(2,1)S(1)}, u32[]{:S(2)}, u32[]{:S(2)}) collective-permute-start(bf16[2,24,2,128]{3,2,1,0:T(2,128)(2,1)S(1)} %get-tuple-element.21), channel_id=1, source_target_pairs={{0,4},{4,8},{8,12},{1,5},{5,9},{9,13},{2,6},{6,10},{10,14},{3,7},{... | collective-permute-start | bytes 73736 | tf_op jit(solution)/shard_map/ppermute | solution.py:21
  22.8 1.3 %collective-permute-start.3 = (bf16[2,24,2,128]{3,2,1,0:T(2,128)(2,1)S(1)}, bf16[2,24,2,128]{3,2,1,0:T(2,128)(2,1)S(1)}, u32[]{:S(2)}, u32[]{:S(2)}) collective-permute-start(bf16[2,24,2,128]{3,2,1,0:T(2,128)(2,1)S(1)} %get-tuple-element.22), channel_id=1, source_target_pairs={{4,0},{8,4},{12,8},{5,1},{9,5},{13,9},{6,2},{10,6},{14,10},{7,3},{... | collective-permute-start | bytes 73736 | tf_op jit(solution)/shard_map/ppermute | solution.py:22
  24.1 0.2 collective-permute-done.2
  24.3 4.2 %collective-permute-done.3 = bf16[2,24,2,128]{3,2,1,0:T(2,128)(2,1)S(1)} collective-permute-done((bf16[2,24,2,128]{3,2,1,0:T(2,128)(2,1)S(1)}, bf16[2,24,2,128]{3,2,1,0:T(2,128)(2,1)S(1)}, u32[]{:S(2)}, u32[]{:S(2)}) %collective-permute-start.3) | collective-permute-done | bytes 24608 | tf_op jit(solution)/shard_map/ppermute | solution.py:22
  28.5 0.1 pad_maximum_fusion
  28.6 0.1 fusion.94
  28.7 2.6 %collective-permute-start.4 = (bf16[2,24,12,2]{3,2,1,0:T(8,128)(2,1)S(1)}, bf16[2,24,12,2]{3,2,1,0:T(8,128)(2,1)S(1)}, u32[]{:S(2)}, u32[]{:S(2)}) collective-permute-start(bf16[2,24,12,2]{3,2,1,0:T(8,128)(2,1)S(1)} %get-tuple-element.20), channel_id=1, source_target_pairs={{0,2},{1,3},{4,6},{5,7},{8,10},{9,11},{12,14},{13,15},{16,18},{17,... | collective-permute-start | bytes 6920 | tf_op jit(solution)/shard_map/ppermute | solution.py:21
  31.4 1.3 %collective-permute-start.5 = (bf16[2,24,12,2]{3,2,1,0:T(8,128)(2,1)S(1)}, bf16[2,24,12,2]{3,2,1,0:T(8,128)(2,1)S(1)}, u32[]{:S(2)}, u32[]{:S(2)}) collective-permute-start(bf16[2,24,12,2]{3,2,1,0:T(8,128)(2,1)S(1)} %get-tuple-element.19), channel_id=1, source_target_pairs={{2,0},{3,1},{6,4},{7,5},{10,8},{11,9},{14,12},{15,13},{18,16},{19,... | collective-permute-start | bytes 6920 | tf_op jit(solution)/shard_map/ppermute | solution.py:22
  32.7 0.1 broadcast_and_fusion
  32.8 0.0 copy-done.5
  32.8 1.8 %all-gather = f32[2,1,128]{2,1,0:T(1,128)S(1)} all-gather(f32[1,1,128]{2,1,0:T(1,128)S(1)} %bitcast.167), channel_id=1, replica_groups=mesh['ens'=2,'row'=4,'col'=2,'chan'=2] {'chan'}, dimensions={0}, use_global_device_ids=true | all-gather | bytes 1536 | tf_op jit(solution)/shard_map/all_gather | solution.py:113
  34.6 0.0 copy-done.4
  34.6 1.8 %all_gather.14 = bf16[12,256]{1,0:T(8,128)(2,1)S(1)} all-gather(bf16[12,128]{1,0:T(8,128)(2,1)S(1)} %copy-done.4), channel_id=1, replica_groups=mesh['ens'=2,'row'=4,'col'=2,'chan'=2] {'chan'}, dimensions={1}, use_global_device_ids=true | all-gather | bytes 9216 | tf_op jit(solution)/shard_map/all_gather | solution.py:111
  36.4 0.0 collective-permute-done.4
  36.4 2.6 %collective-permute-done.5 = bf16[2,24,12,2]{3,2,1,0:T(8,128)(2,1)S(1)} collective-permute-done((bf16[2,24,12,2]{3,2,1,0:T(8,128)(2,1)S(1)}, bf16[2,24,12,2]{3,2,1,0:T(8,128)(2,1)S(1)}, u32[]{:S(2)}, u32[]{:S(2)}) %collective-permute-start.5) | collective-permute-done | bytes 2336 | tf_op jit(solution)/shard_map/ppermute | solution.py:22
  39.0 0.6 %fusion.21 = bf16[2,24,12,68]{3,2,1,0:T(8,128)(2,1)S(1)} fusion(s32[]{:T(128)S(6)} %select_n.69, bf16[2,24,12,2]{3,2,1,0:T(8,128)(2,1)S(1)} %collective-permute-done.4, bf16[2,24,2,128]{3,2,1,0:T(2,128)(2,1)S(1)} %collective-permute-done.2, bf16[2,12,8,128]{3,2,1,0:T(8,128)(2,1)S(1)} %convert.7, bf16[2,12,8,128]{3,2,1,0:T(8,128)(2,1)S(1)} %add.314, ...), kind=kLoop, calls=%fused_computation.39 | loop fusion | flops 470016 | bytes 230404 | tf_op jit(solution)/shard_map/concatenate | solution.py:23
  39.6 0.0 copy-start.2
  39.6 0.5 fusion.93
  40.1 0.4 copy-done.2
  40.5 0.4 fusion.26
  40.9 0.4 fusion.28
  41.3 0.4 fusion.30
  41.7 0.4 fusion.32
  42.1 0.4 fusion.34
  42.5 0.4 fusion.36
  42.9 0.4 fusion.38
  43.3 0.4 fusion.40
  43.7 1.0 %fusion.4 = bf16[2,256,10,66]{1,3,2,0:T(8,128)(2,1)S(1)} fusion(f32[2,10,66,256]{3,2,1,0:T(8,128)S(1)} %fusion.26, f32[2,10,66,256]{3,2,1,0:T(8,128)S(1)} %fusion.28, f32[2,10,66,256]{3,2,1,0:T(8,128)S(1)} %fusion.30, f32[2,10,66,256]{3,2,1,0:T(8,128)S(1)} %fusion.32, f32[2,10,66,256]{3,2,1,0:T(8,128)S(1)} %fusion.34, f32[2,10,66,256]{3,2,1,0:T(8,128)S(1)} %fusion.36, ...), kind=kOutput, calls=%fused_computation.6 | convolution fusion | flops 21288960 | bytes 12685312 | tf_op jit(solution)/shard_map/oi,siyx->soyx/dot_general | solution.py:54
  44.8 0.0 all-gather.3.cloned.1.call-done
  44.8 0.0 copy-start
  44.8 1.3 %fusion.16 = f32[2,8,64,256]{3,2,1,0:T(8,128)S(1)} fusion(bf16[2,256,10,66]{1,3,2,0:T(8,128)(2,1)S(1)} %fusion.4, bf16[9,256,256]{2,1,0:T(8,128)(2,1)} %all-gather.3.cloned.1.call-done), kind=kOutput, calls=%fused_computation.28 | convolution fusion | flops 134217728 | bytes 1703936 | tf_op jit(solution)/shard_map/oi,siyx->soyx/dot_general | solution.py:54
  46.2 0.0 copy-done
  46.2 0.3 convolution_add_fusion.7
  46.5 0.4 convolution_add_fusion.6
  46.9 0.3 convolution_add_fusion.5
  47.2 0.4 convolution_add_fusion.4
  47.6 0.3 convolution_add_fusion.3
  47.9 0.3 convolution_add_fusion.2
  48.3 0.4 convolution_add_fusion.1
  48.6 0.7 %convolution_bitcast_fusion = f32[2,12,8,64]{3,1,2,0:T(8,128)S(1)} fusion(f32[2,8,64,256]{3,2,1,0:T(8,128)S(1)} %convolution_add_fusion.1, bf16[2,256,10,66]{1,3,2,0:T(8,128)(2,1)S(1)} %fusion.4, f32[256]{0:T(256)S(1)} %bitcast.168, bf16[9,256,256]{2,1,0:T(8,128)(2,1)S(1)} %copy-done, bf16[12,256]{1,0:T(8,128)(2,1)S(1)} %all_gather.14), kind=kOutput, calls=%fused_computation.17 | convolution fusion | flops 142344192 | bytes 1762304 | tf_op jit(solution)/shard_map/ko,soyx->skyx/dot_general | solution.py:133
  49.3 0.3 copy.42
  49.7 0.0 copy-start.1
  49.7 0.0 copy-start.3
  49.7 2.7 %all_gather.15 = f32[2,12,8,128]{1,2,0,3:T(8,128)S(1)} all-gather(f32[2,12,8,64]{1,2,0,3:T(8,128)S(1)} %copy.42), channel_id=1, replica_groups=mesh['ens'=2,'row'=4,'col'=2,'chan'=2] {'chan'}, dimensions={3}, use_global_device_ids=true | all-gather | bytes 147456 | tf_op jit(solution)/shard_map/all_gather | solution.py:134
  52.4 0.4 copy.43
  52.8 0.0 copy-done.1
  52.8 0.0 copy-done.3
  52.8 0.8 %add_divide_fusion = (f32[2,12,8,128]{3,2,1,0:T(8,128)}, f32[2,12,8,128]{3,2,1,0:T(8,128)}) fusion(f32[2,12,8,128]{3,2,1,0:T(8,128)S(1)} %copy-done.3, f32[2]{0:T(128)S(1)} %get-tuple-element.6, f32[2]{0:T(128)S(1)} %get-tuple-element.7, f32[2,12,8,128]{3,2,1,0:T(8,128)S(1)} %copy.43, f32[2]{0:T(128)S(1)} %get-tuple-element.26, ...), kind=kLoop, calls=%fused_computation.70 | loop fusion | flops 172032 | bytes 540704 | tf_op jit(solution)/shard_map/div | solution.py:143
  (9 shorter events, 0.1 us)
Async XLA Ops:
  7.2 25.6 %copy-start.5 = (f32[128]{0:T(128)S(1)}, f32[128]{0:T(128)}, u32[]{:S(2)}) copy-start(f32[128]{0:T(128)} %param.18) | copy-start | bytes 1540
  7.2 27.4 %copy-start.4 = (bf16[12,128]{1,0:T(8,128)(2,1)S(1)}, bf16[12,128]{1,0:T(8,128)(2,1)}, u32[]{:S(2)}) copy-start(bf16[12,128]{1,0:T(8,128)(2,1)} %param.19) | copy-start | bytes 9220
  7.2 37.6 %all-gather.3.cloned.1.call-start = ((), (), s32[]{:S(2)}) async-start(), calls=%async_computation | async-start | bytes 1769472 | tf_op jit(solution)/shard_map/all_gather | solution.py:110
  8.0 8.8 %collective-permute-start = (f32[12,4,1]{2,0,1:T(8,128)S(1)}, f32[12,4,1]{2,0,1:T(8,128)S(1)}, u32[]{:S(2)}, u32[]{:S(2)}) collective-permute-start(f32[12,4,1]{2,0,1:T(8,128)S(1)} %get-tuple-element.23), channel_id=1, source_target_pairs={{0,2},{1,3},{4,6},{5,7},{8,10},{9,11},{12,14},{13,15},{16,18},{17,... | collective-permute-start | bytes 584 | tf_op jit(solution)/shard_map/ppermute | solution.py:21
  12.9 5.8 %collective-permute-start.1 = (f32[12,4,1]{2,0,1:T(8,128)S(1)}, f32[12,4,1]{2,0,1:T(8,128)S(1)}, u32[]{:S(2)}, u32[]{:S(2)}) collective-permute-start(f32[12,4,1]{2,0,1:T(8,128)S(1)} %get-tuple-element.24), channel_id=1, source_target_pairs={{2,0},{3,1},{6,4},{7,5},{10,8},{11,9},{14,12},{15,13},{18,16},{19,... | collective-permute-start | bytes 584 | tf_op jit(solution)/shard_map/ppermute | solution.py:22
  19.3 5.0 %collective-permute-start.2 = (bf16[2,24,2,128]{3,2,1,0:T(2,128)(2,1)S(1)}, bf16[2,24,2,128]{3,2,1,0:T(2,128)(2,1)S(1)}, u32[]{:S(2)}, u32[]{:S(2)}) collective-permute-start(bf16[2,24,2,128]{3,2,1,0:T(2,128)(2,1)S(1)} %get-tuple-element.21), channel_id=1, source_target_pairs={{0,4},{4,8},{8,12},{1,5},{5,9},{9,13},{2,6},{6,10},{10,14},{3,7},{... | collective-permute-start | bytes 73736 | tf_op jit(solution)/shard_map/ppermute | solution.py:21
  22.8 5.7 %collective-permute-start.3 = (bf16[2,24,2,128]{3,2,1,0:T(2,128)(2,1)S(1)}, bf16[2,24,2,128]{3,2,1,0:T(2,128)(2,1)S(1)}, u32[]{:S(2)}, u32[]{:S(2)}) collective-permute-start(bf16[2,24,2,128]{3,2,1,0:T(2,128)(2,1)S(1)} %get-tuple-element.22), channel_id=1, source_target_pairs={{4,0},{8,4},{12,8},{5,1},{9,5},{13,9},{6,2},{10,6},{14,10},{7,3},{... | collective-permute-start | bytes 73736 | tf_op jit(solution)/shard_map/ppermute | solution.py:22
  28.7 7.7 %collective-permute-start.4 = (bf16[2,24,12,2]{3,2,1,0:T(8,128)(2,1)S(1)}, bf16[2,24,12,2]{3,2,1,0:T(8,128)(2,1)S(1)}, u32[]{:S(2)}, u32[]{:S(2)}) collective-permute-start(bf16[2,24,12,2]{3,2,1,0:T(8,128)(2,1)S(1)} %get-tuple-element.20), channel_id=1, source_target_pairs={{0,2},{1,3},{4,6},{5,7},{8,10},{9,11},{12,14},{13,15},{16,18},{17,... | collective-permute-start | bytes 6920 | tf_op jit(solution)/shard_map/ppermute | solution.py:21
  31.4 7.6 %collective-permute-start.5 = (bf16[2,24,12,2]{3,2,1,0:T(8,128)(2,1)S(1)}, bf16[2,24,12,2]{3,2,1,0:T(8,128)(2,1)S(1)}, u32[]{:S(2)}, u32[]{:S(2)}) collective-permute-start(bf16[2,24,12,2]{3,2,1,0:T(8,128)(2,1)S(1)} %get-tuple-element.19), channel_id=1, source_target_pairs={{2,0},{3,1},{6,4},{7,5},{10,8},{11,9},{14,12},{15,13},{18,16},{19,... | collective-permute-start | bytes 6920 | tf_op jit(solution)/shard_map/ppermute | solution.py:22
  39.6 0.9 %copy-start.2 = (bf16[9,256,24]{1,2,0:T(8,128)(2,1)S(1)}, bf16[9,256,24]{1,2,0:T(8,128)(2,1)}, u32[]{:S(2)}) copy-start(bf16[9,256,24]{1,2,0:T(8,128)(2,1)} %param.14) | copy-start | bytes 331780
  44.8 1.3 %copy-start = (bf16[9,256,256]{2,1,0:T(8,128)(2,1)S(1)}, bf16[9,256,256]{2,1,0:T(8,128)(2,1)}, u32[]{:S(2)}) copy-start(bf16[9,256,256]{2,1,0:T(8,128)(2,1)} %all-gather.3.cloned.1.call-done) | copy-start | bytes 3538948
  49.7 3.2 %copy-start.1 = (f32[2,12,8,128]{3,2,1,0:T(8,128)S(1)}, f32[2,12,8,128]{3,2,1,0:T(8,128)}, u32[]{:S(2)}) copy-start(f32[2,12,8,128]{3,2,1,0:T(8,128)} %param.10) | copy-start | bytes 294916
  49.7 3.1 %copy-start.3 = (f32[2,12,8,128]{3,2,1,0:T(8,128)S(1)}, f32[2,12,8,128]{3,2,1,0:T(8,128)}, u32[]{:S(2)}) copy-start(f32[2,12,8,128]{3,2,1,0:T(8,128)} %param.11) | copy-start | bytes 294916
Sparse Core Ops, SparseCore 0:
  14.4 11.6 all-gather.2
where the time goes:
time: 60.9 us; the launch traced here: 60.4 us
  starting transfers between devices  14.9 us (24%)
  between operations  14.4 us (24%)
  matrix products  9.14 us (15%)
  waiting for transfers between devices  8.92 us (15%)
  blocking collectives  6.31 us (10%)
  other arithmetic  4.14 us (7%)
  local copies, waits for them, and re-layouts  2.63 us (4%)
    ppermute x3, starting transfers between devices, extended_2(): before = lax.ppermute(last, axis, up)  11 us
    ppermute x3, waiting for transfers between devices, extended_2(): after = lax.ppermute(initial, axis, down)  8.69 us
    dot_general x17, matrix products, conv_valid(): jnp.einsum('oi,siyx->soyx', weight[3 * offset_row + offset_col], window,...  7.96 us
    ppermute x3, starting transfers between devices, extended_2(): after = lax.ppermute(initial, axis, down)  3.88 us
    all_gather x1, blocking collectives, on_device(): network = lax.all_gather(half_network, 'chan', axis=3, tiled=True)  2.69 us
    all_gather x1, blocking collectives, on_device(): lax.all_gather(weight_out, 'chan', axis=1, tiled=True)  1.83 us
    all_gather x1, blocking collectives, on_device(): bias_full = lax.all_gather(bias_mid, 'chan', axis=0, tiled=True)  1.8 us
  transfers between devices with their start and end apart: 7, of which 4 were waited for; matrix products, arithmetic and copies ran while one was open for 14% of the time, Pallas kernels for 0%

commit v1 on v0

--- a/solution.py
+++ b/solution.py
@@ -131,7 +131,9 @@
         conv_valid(hidden_wide, mid_full, rows_here, half_cols) + bias_full[None, :, None, None]
     ).astype(jnp.bfloat16)
     half_network = jnp.einsum("ko,soyx->skyx", out_full, middle, preferred_element_type=jnp.float32)
-    network = lax.all_gather(half_network, "chan", axis=3, tiled=True)
+    network = jnp.concatenate(
+        lax.all_to_all(jnp.stack([half_network] * lax.axis_size("chan")), "chan", 0, 0), axis=3
+    )
     scale_now = jnp.sqrt(noise_now * noise_now + sigma_data * sigma_data)
     skip_coef = sigma_data * sigma_data / (noise_now * noise_now + sigma_data * sigma_data)
     out_coef = sigma_data * noise_now / scale_now

time: 60.9 us -> 63.4 us (1.041)
  blocking collectives: 6.31 us -> 7.42 us
  other arithmetic: 4.14 us -> 5.12 us
    all_to_all x0 -> x1, blocking collectives: none -> 3.79 us  [on_device(): lax.all_to_all(jnp.stack([half_network] * lax.axis_size('chan')), 'chan',...]
    all_gather x1 -> x0, blocking collectives: 2.69 us -> none  [on_device(): network = lax.all_gather(half_network, 'chan', axis=3, tiled=True)]
    all_to_all x0 -> x1, other arithmetic: none -> 0.94 us  [on_device(): lax.all_to_all(jnp.stack([half_network] * lax.axis_size('chan')), 'chan',...]
    unnamed x13 -> x15, local copies, waits for them, and re-layouts: 1.2 us -> 1.52 us
where the time goes in v1:
time: 63.4 us; the launch traced here: 63 us
  starting transfers between devices  14.9 us (24%)
  between operations  14.4 us (23%)
  matrix products  9.14 us (14%)
  waiting for transfers between devices  8.92 us (14%)
  blocking collectives  7.42 us (12%)
  other arithmetic  5.12 us (8%)
  local copies, waits for them, and re-layouts  3.06 us (5%)
    ppermute x3, starting transfers between devices, extended_2(): before = lax.ppermute(last, axis, up)  11 us
    ppermute x3, waiting for transfers between devices, extended_2(): after = lax.ppermute(initial, axis, down)  8.69 us
    dot_general x17, matrix products, conv_valid(): jnp.einsum('oi,siyx->soyx', weight[3 * offset_row + offset_col], window,...  7.96 us
    ppermute x3, starting transfers between devices, extended_2(): after = lax.ppermute(initial, axis, down)  3.88 us
    all_to_all x1, blocking collectives, on_device(): lax.all_to_all(jnp.stack([half_network] * lax.axis_size('chan')), 'chan',...  3.79 us
    all_gather x1, blocking collectives, on_device(): lax.all_gather(weight_out, 'chan', axis=1, tiled=True)  1.83 us
    all_gather x1, blocking collectives, on_device(): bias_full = lax.all_gather(bias_mid, 'chan', axis=0, tiled=True)  1.8 us
    unnamed x15, local copies, waits for them, and re-layouts  1.52 us
  transfers between devices with their start and end apart: 7, of which 4 were waited for; matrix products, arithmetic and copies ran while one was open for 14% of the time, Pallas kernels for 0%

profile of v1, /device:TPU:0, one launch (start us, length us, event | category | flops | bytes accessed | tf_op | source)
XLA Modules:
  0.0 63.0 jit_solution(5564194359743422021)
XLA Ops:
  7.2 0.0 copy-start.5
  7.2 0.0 copy-start.4
  7.2 0.0 all-gather.3.cloned.1.call-start
  7.2 0.7 %copy.25 = f32[12,4,16]{2,0,1:T(8,128)S(1)} copy(f32[12,4,16]{2,1,0:T(4,128)} %param.13) | data formatting | bytes 6144 | tf_op args[3]
  8.0 0.1 fusion.95
  8.0 4.9 %collective-permute-start = (f32[12,4,1]{2,0,1:T(8,128)S(1)}, f32[12,4,1]{2,0,1:T(8,128)S(1)}, u32[]{:S(2)}, u32[]{:S(2)}) collective-permute-start(f32[12,4,1]{2,0,1:T(8,128)S(1)} %get-tuple-element.19), channel_id=1, source_target_pairs={{0,2},{1,3},{4,6},{5,7},{8,10},{9,11},{12,14},{13,15},{16,18},{17,... | collective-permute-start | bytes 584 | tf_op jit(solution)/shard_map/ppermute | solution.py:21
  12.9 1.3 %collective-permute-start.1 = (f32[12,4,1]{2,0,1:T(8,128)S(1)}, f32[12,4,1]{2,0,1:T(8,128)S(1)}, u32[]{:S(2)}, u32[]{:S(2)}) collective-permute-start(f32[12,4,1]{2,0,1:T(8,128)S(1)} %get-tuple-element.20), channel_id=1, source_target_pairs={{2,0},{3,1},{6,4},{7,5},{10,8},{11,9},{14,12},{15,13},{18,16},{19,... | collective-permute-start | bytes 584 | tf_op jit(solution)/shard_map/ppermute | solution.py:22
  14.2 0.0 all-gather.3.cloned.1.call-update
  14.4 0.8 %add_sqrt_fusion = (f32[2]{0:T(128)S(1)}, f32[2]{0:T(128)S(1)}, f32[2]{0:T(128)S(1)}, f32[2]{0:T(128)S(1)}, f32[2]{0:T(128)S(1)}) fusion(s32[2]{0:T(128)} %param.12), kind=kLoop, calls=%fused_computation.140 | loop fusion | flops 34 | bytes 48 | tf_op jit(solution)/shard_map/sqrt | solution.py:144
  15.1 0.8 %multiply_add_fusion.1 = f32[2,256]{1,0:T(2,128)S(1)} fusion(f32[256]{0:T(256)} %param.16, f32[256]{0:T(256)} %param.15, f32[2]{0:T(128)S(1)} %get-tuple-element.21), kind=kLoop, calls=%fused_computation.116 | loop fusion | flops 1024 | bytes 4104 | tf_op jit(solution)/shard_map/add | solution.py:106
  15.9 0.9 %convert.7 = bf16[2,12,8,128]{3,2,1,0:T(8,128)(2,1)S(1)} convert(f32[2,12,8,128]{3,2,1,0:T(8,128)} %param.10) | non-fusion elementwise | flops 24576 | bytes 147456 | tf_op jit(solution)/shard_map/convert
  16.8 0.0 collective-permute-done
  16.8 1.9 %collective-permute-done.1 = f32[12,4,1]{2,0,1:T(8,128)S(1)} collective-permute-done((f32[12,4,1]{2,0,1:T(8,128)S(1)}, f32[12,4,1]{2,0,1:T(8,128)S(1)}, u32[]{:S(2)}, u32[]{:S(2)}) %collective-permute-start.1) | collective-permute-done | bytes 224 | tf_op jit(solution)/shard_map/ppermute | solution.py:22
  18.7 0.2 fusion.42
  19.0 0.2 fusion.96
  19.3 3.5 %collective-permute-start.2 = (bf16[2,24,2,128]{3,2,1,0:T(2,128)(2,1)S(1)}, bf16[2,24,2,128]{3,2,1,0:T(2,128)(2,1)S(1)}, u32[]{:S(2)}, u32[]{:S(2)}) collective-permute-start(bf16[2,24,2,128]{3,2,1,0:T(2,128)(2,1)S(1)} %get-tuple-element.17), channel_id=1, source_target_pairs={{0,4},{4,8},{8,12},{1,5},{5,9},{9,13},{2,6},{6,10},{10,14},{3,7},{... | collective-permute-start | bytes 73736 | tf_op jit(solution)/shard_map/ppermute | solution.py:21
  22.8 1.3 %collective-permute-start.3 = (bf16[2,24,2,128]{3,2,1,0:T(2,128)(2,1)S(1)}, bf16[2,24,2,128]{3,2,1,0:T(2,128)(2,1)S(1)}, u32[]{:S(2)}, u32[]{:S(2)}) collective-permute-start(bf16[2,24,2,128]{3,2,1,0:T(2,128)(2,1)S(1)} %get-tuple-element.18), channel_id=1, source_target_pairs={{4,0},{8,4},{12,8},{5,1},{9,5},{13,9},{6,2},{10,6},{14,10},{7,3},{... | collective-permute-start | bytes 73736 | tf_op jit(solution)/shard_map/ppermute | solution.py:22
  24.1 0.2 collective-permute-done.2
  24.3 4.2 %collective-permute-done.3 = bf16[2,24,2,128]{3,2,1,0:T(2,128)(2,1)S(1)} collective-permute-done((bf16[2,24,2,128]{3,2,1,0:T(2,128)(2,1)S(1)}, bf16[2,24,2,128]{3,2,1,0:T(2,128)(2,1)S(1)}, u32[]{:S(2)}, u32[]{:S(2)}) %collective-permute-start.3) | collective-permute-done | bytes 24608 | tf_op jit(solution)/shard_map/ppermute | solution.py:22
  28.5 0.1 pad_maximum_fusion.1
  28.6 0.1 fusion.94
  28.7 2.6 %collective-permute-start.4 = (bf16[2,24,12,2]{3,2,1,0:T(8,128)(2,1)S(1)}, bf16[2,24,12,2]{3,2,1,0:T(8,128)(2,1)S(1)}, u32[]{:S(2)}, u32[]{:S(2)}) collective-permute-start(bf16[2,24,12,2]{3,2,1,0:T(8,128)(2,1)S(1)} %get-tuple-element.16), channel_id=1, source_target_pairs={{0,2},{1,3},{4,6},{5,7},{8,10},{9,11},{12,14},{13,15},{16,18},{17,... | collective-permute-start | bytes 6920 | tf_op jit(solution)/shard_map/ppermute | solution.py:21
  31.4 1.3 %collective-permute-start.5 = (bf16[2,24,12,2]{3,2,1,0:T(8,128)(2,1)S(1)}, bf16[2,24,12,2]{3,2,1,0:T(8,128)(2,1)S(1)}, u32[]{:S(2)}, u32[]{:S(2)}) collective-permute-start(bf16[2,24,12,2]{3,2,1,0:T(8,128)(2,1)S(1)} %get-tuple-element.15), channel_id=1, source_target_pairs={{2,0},{3,1},{6,4},{7,5},{10,8},{11,9},{14,12},{15,13},{18,16},{19,... | collective-permute-start | bytes 6920 | tf_op jit(solution)/shard_map/ppermute | solution.py:22
  32.7 0.1 broadcast_and_fusion
  32.8 0.0 copy-done.5
  32.8 1.8 %all-gather = f32[2,1,128]{2,1,0:T(1,128)S(1)} all-gather(f32[1,1,128]{2,1,0:T(1,128)S(1)} %bitcast.171), channel_id=1, replica_groups=mesh['ens'=2,'row'=4,'col'=2,'chan'=2] {'chan'}, dimensions={0}, use_global_device_ids=true | all-gather | bytes 1536 | tf_op jit(solution)/shard_map/all_gather | solution.py:113
  34.6 0.0 copy-done.4
  34.6 1.8 %all_gather.11 = bf16[12,256]{1,0:T(8,128)(2,1)S(1)} all-gather(bf16[12,128]{1,0:T(8,128)(2,1)S(1)} %copy-done.4), channel_id=1, replica_groups=mesh['ens'=2,'row'=4,'col'=2,'chan'=2] {'chan'}, dimensions={1}, use_global_device_ids=true | all-gather | bytes 9216 | tf_op jit(solution)/shard_map/all_gather | solution.py:111
  36.4 0.0 collective-permute-done.4
  36.4 2.6 %collective-permute-done.5 = bf16[2,24,12,2]{3,2,1,0:T(8,128)(2,1)S(1)} collective-permute-done((bf16[2,24,12,2]{3,2,1,0:T(8,128)(2,1)S(1)}, bf16[2,24,12,2]{3,2,1,0:T(8,128)(2,1)S(1)}, u32[]{:S(2)}, u32[]{:S(2)}) %collective-permute-start.5) | collective-permute-done | bytes 2336 | tf_op jit(solution)/shard_map/ppermute | solution.py:22
  39.0 0.6 %fusion.21 = bf16[2,24,12,68]{3,2,1,0:T(8,128)(2,1)S(1)} fusion(s32[]{:T(128)S(6)} %select_n.69, bf16[2,24,12,2]{3,2,1,0:T(8,128)(2,1)S(1)} %collective-permute-done.4, bf16[2,24,2,128]{3,2,1,0:T(2,128)(2,1)S(1)} %collective-permute-done.2, bf16[2,12,8,128]{3,2,1,0:T(8,128)(2,1)S(1)} %convert.7, bf16[2,12,8,128]{3,2,1,0:T(8,128)(2,1)S(1)} %add.314, ...), kind=kLoop, calls=%fused_computation.40 | loop fusion | flops 470016 | bytes 230404 | tf_op jit(solution)/shard_map/concatenate | solution.py:23
  39.6 0.0 copy-start.2
  39.6 0.5 fusion.93
  40.1 0.4 copy-done.2
  40.5 0.4 fusion.26
  40.9 0.4 fusion.28
  41.3 0.4 fusion.30
  41.7 0.4 fusion.32
  42.1 0.4 fusion.34
  42.5 0.4 fusion.36
  42.9 0.4 fusion.38
  43.3 0.4 fusion.40
  43.7 1.0 %fusion.4 = bf16[2,256,10,66]{1,3,2,0:T(8,128)(2,1)S(1)} fusion(f32[2,10,66,256]{3,2,1,0:T(8,128)S(1)} %fusion.26, f32[2,10,66,256]{3,2,1,0:T(8,128)S(1)} %fusion.28, f32[2,10,66,256]{3,2,1,0:T(8,128)S(1)} %fusion.30, f32[2,10,66,256]{3,2,1,0:T(8,128)S(1)} %fusion.32, f32[2,10,66,256]{3,2,1,0:T(8,128)S(1)} %fusion.34, f32[2,10,66,256]{3,2,1,0:T(8,128)S(1)} %fusion.36, ...), kind=kOutput, calls=%fused_computation.6 | convolution fusion | flops 21288960 | bytes 12685312 | tf_op jit(solution)/shard_map/oi,siyx->soyx/dot_general | solution.py:54
  44.8 0.0 all-gather.3.cloned.1.call-done
  44.8 0.0 copy-start
  44.8 1.3 %fusion.16 = f32[2,8,64,256]{3,2,1,0:T(8,128)S(1)} fusion(bf16[2,256,10,66]{1,3,2,0:T(8,128)(2,1)S(1)} %fusion.4, bf16[9,256,256]{2,1,0:T(8,128)(2,1)} %all-gather.3.cloned.1.call-done), kind=kOutput, calls=%fused_computation.28 | convolution fusion | flops 134217728 | bytes 1703936 | tf_op jit(solution)/shard_map/oi,siyx->soyx/dot_general | solution.py:54
  46.2 0.3 convolution_add_fusion.7
  46.5 0.4 convolution_add_fusion.6
  46.9 0.3 convolution_add_fusion.5
  47.2 0.4 convolution_add_fusion.4
  47.6 0.3 convolution_add_fusion.3
  47.9 0.3 convolution_add_fusion.2
  48.3 0.4 convolution_add_fusion.1
  48.6 0.7 %convolution_bitcast_fusion = f32[1,2,12,8,64]{4,2,3,1,0:T(8,128)S(1)} fusion(f32[2,8,64,256]{3,2,1,0:T(8,128)S(1)} %convolution_add_fusion.1, bf16[2,256,10,66]{1,3,2,0:T(8,128)(2,1)S(1)} %fusion.4, f32[256]{0:T(256)S(1)} %bitcast.172, bf16[9,256,256]{2,1,0:T(8,128)(2,1)S(1)} %copy-done, bf16[12,256]{1,0:T(8,128)(2,1)S(1)} %all_gather.11), kind=kOutput, calls=%fused_computation.17 | convolution fusion | flops 142344192 | bytes 1762304 | tf_op jit(solution)/shard_map/ko,soyx->skyx/dot_general | solution.py:133
  49.4 0.1 copy.38
  49.4 0.2 reshape.180
  49.6 3.8 %all_to_all.5 = f32[2,1,12288]{2,1,0:T(1,128)S(1)} all-to-all(f32[2,1,12288]{2,1,0:T(1,128)S(1)} %reshape.180), channel_id=1, replica_groups=mesh['ens'=2,'row'=4,'col'=2,'chan'=2] {'chan'}, dimensions={0} | all-to-all | bytes 196608 | tf_op jit(solution)/shard_map/all_to_all | solution.py:135
  53.4 0.5 broadcast.638
  53.9 0.9 %reduce = f32[2,12288]{1,0:T(2,128)S(1)} reduce(f32[2,1,12288]{2,1,0:T(1,128)S(1)} %all_to_all.5, f32[]{:T(128)} %broadcast.638), dimensions={1}, to_apply=%all_to_all.3.reduce_sub_computation | reduce | bytes 196612 | tf_op jit(solution)/shard_map/all_to_all | solution.py:135
  54.8 0.2 reshape.181
  55.0 0.2 copy.39
  55.2 0.2 reshape.156
  55.3 0.0 copy-done.1
  55.3 0.8 %add_divide_fusion = (f32[2,12,8,128]{3,2,1,0:T(8,128)}, f32[2,12,8,128]{3,2,1,0:T(8,128)}) fusion(f32[2,12,8,128]{3,2,1,0:T(8,128)S(1)} %copy-done.3, f32[2]{0:T(128)S(1)} %get-tuple-element.2, f32[2]{0:T(128)S(1)} %get-tuple-element.3, f32[2,12,8,128]{3,2,1,0:T(8,128)S(1)} %reshape.156, f32[2]{0:T(128)S(1)} %get-tuple-element.22, ...), kind=kLoop, calls=%fused_computation.71 | loop fusion | flops 172032 | bytes 540704 | tf_op jit(solution)/shard_map/div | solution.py:145
  (14 shorter events, 0.2 us)
Async XLA Ops:
  7.2 25.6 %copy-start.5 = (f32[128]{0:T(128)S(1)}, f32[128]{0:T(128)}, u32[]{:S(2)}) copy-start(f32[128]{0:T(128)} %param.18) | copy-start | bytes 1540
  7.2 27.4 %copy-start.4 = (bf16[12,128]{1,0:T(8,128)(2,1)S(1)}, bf16[12,128]{1,0:T(8,128)(2,1)}, u32[]{:S(2)}) copy-start(bf16[12,128]{1,0:T(8,128)(2,1)} %param.19) | copy-start | bytes 9220
  7.2 37.6 %all-gather.3.cloned.1.call-start = ((), (), s32[]{:S(2)}) async-start(), calls=%async_computation.1 | async-start | bytes 1769472 | tf_op jit(solution)/shard_map/all_gather | solution.py:110
  8.0 8.8 %collective-permute-start = (f32[12,4,1]{2,0,1:T(8,128)S(1)}, f32[12,4,1]{2,0,1:T(8,128)S(1)}, u32[]{:S(2)}, u32[]{:S(2)}) collective-permute-start(f32[12,4,1]{2,0,1:T(8,128)S(1)} %get-tuple-element.19), channel_id=1, source_target_pairs={{0,2},{1,3},{4,6},{5,7},{8,10},{9,11},{12,14},{13,15},{16,18},{17,... | collective-permute-start | bytes 584 | tf_op jit(solution)/shard_map/ppermute | solution.py:21
  12.9 5.8 %collective-permute-start.1 = (f32[12,4,1]{2,0,1:T(8,128)S(1)}, f32[12,4,1]{2,0,1:T(8,128)S(1)}, u32[]{:S(2)}, u32[]{:S(2)}) collective-permute-start(f32[12,4,1]{2,0,1:T(8,128)S(1)} %get-tuple-element.20), channel_id=1, source_target_pairs={{2,0},{3,1},{6,4},{7,5},{10,8},{11,9},{14,12},{15,13},{18,16},{19,... | collective-permute-start | bytes 584 | tf_op jit(solution)/shard_map/ppermute | solution.py:22
  19.3 5.0 %collective-permute-start.2 = (bf16[2,24,2,128]{3,2,1,0:T(2,128)(2,1)S(1)}, bf16[2,24,2,128]{3,2,1,0:T(2,128)(2,1)S(1)}, u32[]{:S(2)}, u32[]{:S(2)}) collective-permute-start(bf16[2,24,2,128]{3,2,1,0:T(2,128)(2,1)S(1)} %get-tuple-element.17), channel_id=1, source_target_pairs={{0,4},{4,8},{8,12},{1,5},{5,9},{9,13},{2,6},{6,10},{10,14},{3,7},{... | collective-permute-start | bytes 73736 | tf_op jit(solution)/shard_map/ppermute | solution.py:21
  22.8 5.7 %collective-permute-start.3 = (bf16[2,24,2,128]{3,2,1,0:T(2,128)(2,1)S(1)}, bf16[2,24,2,128]{3,2,1,0:T(2,128)(2,1)S(1)}, u32[]{:S(2)}, u32[]{:S(2)}) collective-permute-start(bf16[2,24,2,128]{3,2,1,0:T(2,128)(2,1)S(1)} %get-tuple-element.18), channel_id=1, source_target_pairs={{4,0},{8,4},{12,8},{5,1},{9,5},{13,9},{6,2},{10,6},{14,10},{7,3},{... | collective-permute-start | bytes 73736 | tf_op jit(solution)/shard_map/ppermute | solution.py:22
  28.7 7.7 %collective-permute-start.4 = (bf16[2,24,12,2]{3,2,1,0:T(8,128)(2,1)S(1)}, bf16[2,24,12,2]{3,2,1,0:T(8,128)(2,1)S(1)}, u32[]{:S(2)}, u32[]{:S(2)}) collective-permute-start(bf16[2,24,12,2]{3,2,1,0:T(8,128)(2,1)S(1)} %get-tuple-element.16), channel_id=1, source_target_pairs={{0,2},{1,3},{4,6},{5,7},{8,10},{9,11},{12,14},{13,15},{16,18},{17,... | collective-permute-start | bytes 6920 | tf_op jit(solution)/shard_map/ppermute | solution.py:21
  31.4 7.6 %collective-permute-start.5 = (bf16[2,24,12,2]{3,2,1,0:T(8,128)(2,1)S(1)}, bf16[2,24,12,2]{3,2,1,0:T(8,128)(2,1)S(1)}, u32[]{:S(2)}, u32[]{:S(2)}) collective-permute-start(bf16[2,24,12,2]{3,2,1,0:T(8,128)(2,1)S(1)} %get-tuple-element.15), channel_id=1, source_target_pairs={{2,0},{3,1},{6,4},{7,5},{10,8},{11,9},{14,12},{15,13},{18,16},{19,... | collective-permute-start | bytes 6920 | tf_op jit(solution)/shard_map/ppermute | solution.py:22
  39.6 0.9 %copy-start.2 = (bf16[9,256,24]{1,2,0:T(8,128)(2,1)S(1)}, bf16[9,256,24]{1,2,0:T(8,128)(2,1)}, u32[]{:S(2)}) copy-start(bf16[9,256,24]{1,2,0:T(8,128)(2,1)} %param.14) | copy-start | bytes 331780
  44.8 1.3 %copy-start = (bf16[9,256,256]{2,1,0:T(8,128)(2,1)S(1)}, bf16[9,256,256]{2,1,0:T(8,128)(2,1)}, u32[]{:S(2)}) copy-start(bf16[9,256,256]{2,1,0:T(8,128)(2,1)} %all-gather.3.cloned.1.call-done) | copy-start | bytes 3538948
  49.3 6.0 %copy-start.1 = (f32[2,12,8,128]{3,2,1,0:T(8,128)S(1)}, f32[2,12,8,128]{3,2,1,0:T(8,128)}, u32[]{:S(2)}) copy-start(f32[2,12,8,128]{3,2,1,0:T(8,128)} %param.10) | copy-start | bytes 294916
  49.3 6.0 %copy-start.3 = (f32[2,12,8,128]{3,2,1,0:T(8,128)S(1)}, f32[2,12,8,128]{3,2,1,0:T(8,128)}, u32[]{:S(2)}) copy-start(f32[2,12,8,128]{3,2,1,0:T(8,128)} %param.11) | copy-start | bytes 294916
Sparse Core Ops, SparseCore 0:
  14.4 11.6 all-gather.2
